TPU v7x, 32 devices: a whole 2x2x4 slice. The times are simulated.
32 devices in a mesh: section: 2 (over y), rows: 4 (over z), heads: 4 (over x, core).
Axes of the slice: x: 2, y: 2, z: 4, core: 2. Of those that a mesh axis runs over, the one named last changes fastest.
Arguments:
- tokens: bfloat16 [2, 2048, 4, 1024], P('section', 'heads', 'rows'), may hold values from -6 to 6
- image_lengths: int32 [2, 4, 6], P(None, 'rows'), may hold values from 64 to 576, as said below
- tile_ranks: int32 [2, 4, 6], P(None, 'rows'), may hold values from 0 to 5, each once within a row
- w_qkv: bfloat16 [1024, 3, 1024], P(None, None, 'heads'), may hold values from -0.1875 to 0.1875
- bias_qv: bfloat16 [2, 1024], P(None, 'heads'), may hold values from -3 to 3
- w_out: bfloat16 [1024, 1024], P('heads'), may hold values from -1.5 to 1.5
- bias_out: bfloat16 [1024], replicated, may hold values from -3 to 3
- w_up: bfloat16 [1024, 4096], P(None, 'heads'), may hold values from -0.1875 to 0.1875
- bias_up: bfloat16 [4096], P('heads'), may hold values from -3 to 3
- w_down: bfloat16 [4096, 1024], P('heads'), may hold values from -0.09375 to 0.09375
- bias_down: bfloat16 [1024], replicated, may hold values from -3 to 3
- ln1_gain: bfloat16 [1024], replicated, may hold values from 0.5 to 1.5
- ln1_bias: bfloat16 [1024], replicated, may hold values from -3 to 3
- ln2_gain: bfloat16 [1024], replicated, may hold values from 0.5 to 1.5
- ln2_bias: bfloat16 [1024], replicated, may hold values from -3 to 3
- grad_out: bfloat16 [2, 2048, 4, 1024], P(None, None, 'rows', ('section', 'heads')), may hold values from -6 to 6
- grad_tap: bfloat16 [2, 2048, 4, 1024], P(None, None, 'rows', ('section', 'heads')), may hold values from -6 to 6
Outputs:
- block_output: bfloat16 [2, 2048, 4, 1024], P(None, None, 'rows', ('section', 'heads'))
- input_tap: bfloat16 [2, 2048, 4, 1024], P(None, None, 'rows', ('section', 'heads'))
- grad_tokens: float32 [2, 2048, 4, 1024], P('section', 'heads', 'rows')
- grad_w_qkv: float32 [1024, 3, 1024], P(None, None, 'heads')
- grad_bias_qv: float32 [2, 1024], P(None, 'heads')
- grad_w_out: float32 [1024, 1024], P('heads')
- grad_bias_out: float32 [1024], replicated
- grad_w_up: float32 [1024, 4096], P(None, 'heads')
- grad_bias_up: float32 [4096], P('heads')
- grad_w_down: float32 [4096, 1024], P('heads')
- grad_bias_down: float32 [1024], replicated
- grad_ln1_gain: float32 [1024], replicated
- grad_ln1_bias: float32 [1024], replicated
- grad_ln2_gain: float32 [1024], replicated
- grad_ln2_bias: float32 [1024], replicated
Inputs may be any that keep to these rules, and one draw needn't show every extreme that they name: `image_lengths`: each row holds the patch counts of the 6 images of one sequence, in packing order, summing to 1920; the remaining positions of the 2048 are padding; every row has an image of exactly 576 patches and one of exactly 64. `tile_ranks`: each row is an ordering of the images 0 to 5: their places in the decoder's order.
All inputs are finite; a program needn't handle non-finite values.
Results may differ from a plain program's by a relative error of at most 0.024.
Values may be sent and summed in bfloat16 or wider, within the bound.
A program may use at most 192 MiB of HBM per device.

v0:
```python
from functools import partial
import jax
import jax.numpy as jnp
from jax import lax
from jax.sharding import PartitionSpec as P

HD = 64
EPSILON = 1e-06
MASKED = -1e30


def layer_norm(values_in, norm_gain, norm_shift):
    average = jnp.mean(values_in, axis=-1, keepdims=True)
    centred = values_in - average
    variance = jnp.mean(centred * centred, axis=-1, keepdims=True)
    return centred * lax.rsqrt(variance + EPSILON) * norm_gain + norm_shift


def gelu_exact(values_in):
    return jax.nn.gelu(values_in, approximate=False)


def image_tables(lengths, tile_order, extent):
    image_ends = jnp.cumsum(lengths)
    image_starts = image_ends - lengths
    earlier = (tile_order[None, :] < tile_order[:, None]).astype(jnp.int32)
    new_starts = jnp.sum(earlier * lengths[None, :], axis=1)
    position = jnp.arange(extent, dtype=jnp.int32)
    segment = jnp.sum((position[:, None] >= image_ends[None, :]).astype(jnp.int32), axis=1)
    inside_new = (position[:, None] >= new_starts[None, :]) & (
        position[:, None] < (new_starts + lengths)[None, :]
    )
    source = position + jnp.sum(jnp.where(inside_new, image_starts - new_starts, 0), axis=1)
    inside_old = segment[:, None] == jnp.arange(lengths.shape[0], dtype=jnp.int32)[None, :]
    target = position + jnp.sum(jnp.where(inside_old, new_starts - image_starts, 0), axis=1)
    return (segment, source, target)


def reorder_pair(first_rows, second_rows, picks):
    extent = picks.shape[-1]
    columns = jnp.arange(extent, dtype=jnp.int32)
    selector = (picks[..., None] == columns).astype(jnp.bfloat16)
    first_out = jnp.einsum(
        "hspq,hqsc->hpsc", selector, first_rows, preferred_element_type=jnp.float32
    )
    second_out = jnp.einsum(
        "hspq,hqsc->hpsc", selector, second_rows, preferred_element_type=jnp.float32
    )
    return (first_out.astype(jnp.bfloat16), second_out.astype(jnp.bfloat16))


def masked_scores(queries, key_seq, segment_rows, segment_seq):
    scores = jnp.einsum(
        "qhd,khd->hqk", queries, key_seq, preferred_element_type=jnp.float32
    ) * HD ** (-0.5)
    allowed = segment_rows[:, None] == segment_seq[None, :]
    return jnp.where(allowed[None], scores, MASKED)


def attend_forward(query_seq, key_seq, value_seq, segment_seq, block_rows):
    extent = query_seq.shape[0]
    block_count = extent // block_rows
    query_blocks = query_seq.reshape((block_count, block_rows) + query_seq.shape[1:])
    segment_blocks = segment_seq.reshape(block_count, block_rows)

    def one_block(block_item):
        queries, segment_rows = block_item
        scores = masked_scores(queries, key_seq, segment_rows, segment_seq)
        row_max = jnp.max(scores, axis=-1, keepdims=True)
        exponent = jnp.exp(scores - row_max)
        row_total = jnp.sum(exponent, axis=-1, keepdims=True)
        attend_prob = (exponent / row_total).astype(jnp.bfloat16)
        mixture = jnp.einsum(
            "hqk,khd->qhd", attend_prob, value_seq, preferred_element_type=jnp.float32
        )
        return (mixture, (row_max + jnp.log(row_total))[..., 0])

    mixture, log_sum = lax.map(one_block, (query_blocks, segment_blocks))
    return (mixture.reshape(query_seq.shape), log_sum)


def attend_backward(query_seq, key_seq, value_seq, segment_seq, log_sum, grad_seq, block_rows):
    extent = query_seq.shape[0]
    block_count = extent // block_rows
    query_blocks = query_seq.reshape((block_count, block_rows) + query_seq.shape[1:])
    grad_blocks = grad_seq.reshape((block_count, block_rows) + grad_seq.shape[1:])
    segment_blocks = segment_seq.reshape(block_count, block_rows)

    def one_block(running, block_item):
        key_acc, value_acc = running
        queries, segment_rows, log_rows, grad_rows = block_item
        scores = masked_scores(queries, key_seq, segment_rows, segment_seq)
        attend_prob = jnp.exp(scores - log_rows[..., None])
        prob_low = attend_prob.astype(jnp.bfloat16)
        grad_prob = jnp.einsum(
            "qhd,khd->hqk", grad_rows, value_seq, preferred_element_type=jnp.float32
        )
        inner = jnp.sum(attend_prob * grad_prob, axis=-1, keepdims=True)
        grad_score = (attend_prob * (grad_prob - inner) * HD ** (-0.5)).astype(jnp.bfloat16)
        grad_query = jnp.einsum(
            "hqk,khd->qhd", grad_score, key_seq, preferred_element_type=jnp.float32
        )
        key_acc = key_acc + jnp.einsum(
            "hqk,qhd->khd", grad_score, queries, preferred_element_type=jnp.float32
        )
        value_acc = value_acc + jnp.einsum(
            "hqk,qhd->khd", prob_low, grad_rows, preferred_element_type=jnp.float32
        )
        return ((key_acc, value_acc), grad_query)

    zero_rows = jnp.zeros(key_seq.shape, jnp.float32)
    (grad_key, grad_value), grad_query = lax.scan(
        one_block, (zero_rows, zero_rows), (query_blocks, segment_blocks, log_sum, grad_blocks)
    )
    return (grad_query.reshape(query_seq.shape), grad_key, grad_value)


def per_device(
    tokens,
    image_lengths,
    tile_ranks,
    w_qkv,
    bias_qv,
    w_out,
    bias_out,
    w_up,
    bias_up,
    w_down,
    bias_down,
    ln1_gain,
    ln1_bias,
    ln2_gain,
    ln2_bias,
    grad_out,
    grad_tap,
):
    own_tokens = tokens[0]
    part_rows = own_tokens.shape[0]
    seq_count = own_tokens.shape[1]
    full_len = part_rows * lax.axis_size("heads")
    block_rows = min(512, full_len)
    section_at = lax.axis_index("section")
    head_at = lax.axis_index("heads")
    halves = image_lengths.shape[0]
    image_count = image_lengths.shape[2]
    flat_lengths = image_lengths.reshape(halves * seq_count, image_count)
    flat_orders = tile_ranks.reshape(halves * seq_count, image_count)
    segments, sources, targets = jax.vmap(partial(image_tables, extent=full_len))(
        flat_lengths, flat_orders
    )
    segments = segments.reshape(halves, seq_count, full_len)
    sources = sources.reshape(halves, seq_count, full_len)
    targets = targets.reshape(halves, seq_count, full_len)
    own_segments = lax.dynamic_index_in_dim(segments, section_at, 0, keepdims=False)
    row_places = head_at * part_rows + jnp.arange(part_rows, dtype=jnp.int32)
    valid_rows = (
        (jnp.take(own_segments, row_places, axis=1) < image_count).astype(jnp.float32).T[:, :, None]
    )
    token_values = own_tokens.astype(jnp.float32)
    normed_one = layer_norm(token_values, ln1_gain, ln1_bias).astype(jnp.bfloat16)
    gathered_one = lax.all_gather(normed_one, "heads", axis=0, tiled=True)
    projected = jnp.einsum("rsd,dck->rsck", gathered_one, w_qkv, preferred_element_type=jnp.float32)
    query_all = (projected[:, :, 0] + bias_qv[0]).astype(jnp.bfloat16)
    key_all = projected[:, :, 1].astype(jnp.bfloat16)
    value_all = (projected[:, :, 2] + bias_qv[1]).astype(jnp.bfloat16)
    head_groups = query_all.shape[2] // HD
    split_shape = (full_len, seq_count, head_groups, HD)
    query_heads = query_all.reshape(split_shape)
    key_heads = key_all.reshape(split_shape)
    value_heads = value_all.reshape(split_shape)
    which = 0
    mixture, log_sum = attend_forward(
        query_heads[:, which],
        key_heads[:, which],
        value_heads[:, which],
        own_segments[which],
        block_rows,
    )
    mixtures = [mixture]
    log_sums = [log_sum]
    attended = (
        jnp.stack(mixtures, axis=1)
        .reshape(full_len, seq_count, head_groups * HD)
        .astype(jnp.bfloat16)
    )
    picked = attended
    attn_sum = (
        lax.psum_scatter(
            jnp.einsum("rsk,kd->rsd", picked, w_out, preferred_element_type=jnp.float32).astype(
                jnp.bfloat16
            ),
            "heads",
            scatter_dimension=0,
            tiled=True,
        ).astype(jnp.float32)
        + bias_out
    )
    after_attn = token_values + attn_sum
    normed_two = layer_norm(after_attn, ln2_gain, ln2_bias).astype(jnp.bfloat16)
    gathered_two = lax.all_gather(normed_two, "heads", axis=0, tiled=True)
    pre_act = (
        jnp.einsum("rsd,df->rsf", gathered_two, w_up, preferred_element_type=jnp.float32) + bias_up
    )
    activated = gelu_exact(pre_act).astype(jnp.bfloat16)
    picked = activated
    mlp_sum = (
        lax.psum_scatter(
            jnp.einsum("rsf,fd->rsd", picked, w_down, preferred_element_type=jnp.float32).astype(
                jnp.bfloat16
            ),
            "heads",
            scatter_dimension=0,
            tiled=True,
        ).astype(jnp.float32)
        + bias_down
    )
    block_out = ((after_attn + mlp_sum) * valid_rows).astype(jnp.bfloat16)
    sent_out, sent_tap = (
        lax.all_to_all(block_out, ("section", "heads"), split_axis=2, concat_axis=0, tiled=True),
        lax.all_to_all(own_tokens, ("section", "heads"), split_axis=2, concat_axis=0, tiled=True),
    )
    decoder_shape = (halves, full_len, seq_count, sent_out.shape[2])
    output_dec, tap_dec = reorder_pair(
        sent_out.reshape(decoder_shape), sent_tap.reshape(decoder_shape), sources
    )
    encoder_shape = (halves * full_len, seq_count, grad_out.shape[3])
    back_out, back_tap = reorder_pair(grad_out, grad_tap, targets)
    grad_block, grad_direct = (
        lax.all_to_all(
            back_out.reshape(encoder_shape),
            ("section", "heads"),
            split_axis=0,
            concat_axis=2,
            tiled=True,
        ),
        lax.all_to_all(
            back_tap.reshape(encoder_shape),
            ("section", "heads"),
            split_axis=0,
            concat_axis=2,
            tiled=True,
        ),
    )
    grad_mlp_full = grad_block.astype(jnp.float32) * valid_rows
    grad_mlp = grad_mlp_full.astype(jnp.bfloat16)
    grad_b_down = jnp.sum(grad_mlp, axis=(0, 1), dtype=jnp.float32)
    grad_mlp_all = lax.all_gather(grad_mlp, "heads", axis=0, tiled=True)
    grad_w_down_part = jnp.einsum(
        "rsf,rsd->fd", activated, grad_mlp_all, preferred_element_type=jnp.float32
    )
    grad_act = jnp.einsum("rsd,fd->rsf", grad_mlp_all, w_down, preferred_element_type=jnp.float32)
    gelu_back = jax.vjp(gelu_exact, pre_act)[1]
    grad_pre = gelu_back(grad_act)[0].astype(jnp.bfloat16)
    grad_w_up_part = jnp.einsum(
        "rsd,rsf->df", gathered_two, grad_pre, preferred_element_type=jnp.float32
    )
    grad_b_up = jnp.sum(grad_pre, axis=(0, 1), dtype=jnp.float32)
    picked = grad_pre
    grad_normed_two = lax.psum_scatter(
        jnp.einsum("rsf,df->rsd", picked, w_up, preferred_element_type=jnp.float32).astype(
            jnp.bfloat16
        ),
        "heads",
        scatter_dimension=0,
        tiled=True,
    ).astype(jnp.float32)
    norm_two_back = jax.vjp(layer_norm, after_attn, ln2_gain, ln2_bias)[1]
    grad_after, grad_gain_two, grad_shift_two = norm_two_back(grad_normed_two)
    grad_after = grad_after + grad_mlp_full
    grad_attn = grad_after.astype(jnp.bfloat16)
    grad_b_out = jnp.sum(grad_attn, axis=(0, 1), dtype=jnp.float32)
    grad_attn_all = lax.all_gather(grad_attn, "heads", axis=0, tiled=True)
    grad_w_out_part = jnp.einsum(
        "rsk,rsd->kd", attended, grad_attn_all, preferred_element_type=jnp.float32
    )
    grad_attended = (
        jnp.einsum("rsd,kd->rsk", grad_attn_all, w_out, preferred_element_type=jnp.float32)
        .astype(jnp.bfloat16)
        .reshape(split_shape)
    )
    which = 0
    grad_query, grad_key, grad_value = attend_backward(
        query_heads[:, which],
        key_heads[:, which],
        value_heads[:, which],
        own_segments[which],
        log_sums[which],
        grad_attended[:, which],
        block_rows,
    )
    query_grads = [grad_query]
    key_grads = [grad_key]
    value_grads = [grad_value]
    flat_shape = (full_len, seq_count, head_groups * HD)
    grad_query_all = jnp.stack(query_grads, axis=1).reshape(flat_shape).astype(jnp.bfloat16)
    grad_key_all = jnp.stack(key_grads, axis=1).reshape(flat_shape).astype(jnp.bfloat16)
    grad_value_all = jnp.stack(value_grads, axis=1).reshape(flat_shape).astype(jnp.bfloat16)
    grad_projected = jnp.stack([grad_query_all, grad_key_all, grad_value_all], axis=2)
    grad_w_qkv_part = jnp.einsum(
        "rsd,rsck->dck", gathered_one, grad_projected, preferred_element_type=jnp.float32
    )
    grad_b_qv = jnp.stack(
        [
            jnp.sum(grad_query_all, axis=(0, 1), dtype=jnp.float32),
            jnp.sum(grad_value_all, axis=(0, 1), dtype=jnp.float32),
        ]
    )
    picked = grad_projected
    grad_normed_one = lax.psum_scatter(
        jnp.einsum("rsck,dck->rsd", picked, w_qkv, preferred_element_type=jnp.float32).astype(
            jnp.bfloat16
        ),
        "heads",
        scatter_dimension=0,
        tiled=True,
    ).astype(jnp.float32)
    norm_one_back = jax.vjp(layer_norm, token_values, ln1_gain, ln1_bias)[1]
    grad_input, grad_gain_one, grad_shift_one = norm_one_back(grad_normed_one)
    grad_tokens = grad_input + grad_after + grad_direct.astype(jnp.float32)
    (
        grad_w_qkv_part,
        grad_b_qv,
        grad_w_out_part,
        grad_b_out,
        grad_gain_one,
        grad_shift_one,
        grad_w_up_part,
        grad_b_up,
        grad_w_down_part,
        grad_b_down,
        grad_gain_two,
        grad_shift_two,
    ) = (
        lax.psum(grad_w_qkv_part.astype(jnp.bfloat16), ("section", "rows")).astype(jnp.float32),
        lax.psum(grad_b_qv.astype(jnp.bfloat16), ("section", "rows")).astype(jnp.float32),
        lax.psum(grad_w_out_part.astype(jnp.bfloat16), ("section", "rows")).astype(jnp.float32),
        lax.psum(grad_b_out.astype(jnp.bfloat16), ("section", "rows")).astype(jnp.float32),
        lax.psum(grad_gain_one, ("section", "rows")).astype(jnp.float32),
        lax.psum(grad_shift_one, ("section", "rows")).astype(jnp.float32),
        lax.psum(grad_w_up_part.astype(jnp.bfloat16), ("section", "rows")).astype(jnp.float32),
        lax.psum(grad_b_up.astype(jnp.bfloat16), ("section", "rows")).astype(jnp.float32),
        lax.psum(grad_w_down_part.astype(jnp.bfloat16), ("section", "rows")).astype(jnp.float32),
        lax.psum(grad_b_down.astype(jnp.bfloat16), ("section", "rows")).astype(jnp.float32),
        lax.psum(grad_gain_two, ("section", "rows")).astype(jnp.float32),
        lax.psum(grad_shift_two, ("section", "rows")).astype(jnp.float32),
    )
    grad_b_out, grad_b_down, grad_gain_one, grad_shift_one, grad_gain_two, grad_shift_two = (
        lax.psum(
            (grad_b_out, grad_b_down, grad_gain_one, grad_shift_one, grad_gain_two, grad_shift_two),
            "heads",
        )
    )
    return (
        output_dec,
        tap_dec,
        grad_tokens[None],
        grad_w_qkv_part,
        grad_b_qv,
        grad_w_out_part,
        grad_b_out,
        grad_w_up_part,
        grad_b_up,
        grad_w_down_part,
        grad_b_down,
        grad_gain_one,
        grad_shift_one,
        grad_gain_two,
        grad_shift_two,
    )


def solution(mesh):
    placed = (
        P("section", "heads", "rows", None),
        P(None, "rows", None),
        P(None, "rows", None),
        P(None, None, "heads"),
        P(None, "heads"),
        P("heads", None),
        P(),
        P(None, "heads"),
        P("heads"),
        P("heads", None),
        P(),
        P(),
        P(),
        P(),
        P(),
        P(None, None, "rows", ("section", "heads")),
        P(None, None, "rows", ("section", "heads")),
    )
    return jax.shard_map(
        per_device,
        mesh=mesh,
        in_specs=placed,
        out_specs=(
            P(None, None, "rows", ("section", "heads")),
            P(None, None, "rows", ("section", "heads")),
            P("section", "heads", "rows", None),
            P(None, None, "heads"),
            P(None, "heads"),
            P("heads", None),
            P(),
            P(None, "heads"),
            P("heads"),
            P("heads", None),
            P(),
            P(),
            P(),
            P(),
            P(),
        ),
        check_vma=False,
    )
```

profile of v0, /device:TPU:0, one launch (start us, length us, event | category | flops | bytes accessed | tf_op | source)
XLA Modules:
  0.0 1077.3 jit_solution(13621030071722300098)
XLA Ops:
  17.5 35.0 %all-gather.5.cloned.1.call-done = bf16[2048,1,1024]{2,0,1:T(8,128)(2,1)} async-done(((bf16[512,1,1024]{2,0,1:T(8,128)(2,1)}), bf16[2048,1,1024]{2,0,1:T(8,128)(2,1)}) %all-gather.5.cloned.1.call-update) | async-done | bytes 4194320 | tf_op jit(solution)/shard_map/all_gather | solution.py:161
  52.5 5.8 fusion.115
  69.9 62.9 %while.27 = (s32[]{:T(128)}, bf16[4,512,4,64]{1,3,2,0:T(8,128)(2,1)}, f32[4,4,512]{2,1,0:T(4,128)}, s32[4,512]{1,0:T(4,128)S(1)}, s32[1,2048]{1,0:T(1,128)S(1)},...) while((s32[]{:T(128)}, ...), condition=%wide.region_7.8_spmd, body=%wide.region_4.7_spmd.sunk | while | flops 1125120000 | bytes 70072528 | solution.py:78
  70.6 4.5 fusion.230
  75.1 4.4 fusion.231
  79.6 5.1 fusion.232
  86.3 4.5 fusion.230
  90.8 4.4 fusion.231
  95.3 5.1 fusion.232
  102.0 4.5 fusion.230
  106.5 4.4 fusion.231
  111.0 5.1 fusion.232
  117.7 4.5 fusion.230
  122.2 4.4 fusion.231
  126.6 5.1 fusion.232
  139.7 44.5 %reduce-scatter.5.cloned.1.call-done = bf16[512,1,1024]{2,0,1:T(8,128)(2,1)} async-done(((bf16[2048,1,1024]{2,0,1:T(8,128)(2,1)}), bf16[512,1,1024]{2,0,1:T(8,128)(2,1)}) %reduce-scatter.5.cloned.1.call-update) | async-done | bytes 1048592 | tf_op jit(solution)/shard_map/reduce_scatter | solution.py:188
  191.5 7.9 fusion.130
  212.9 22.5 %all-to-all-done.2 = bf16[8,2,32768]{2,1,0:T(2,128)(2,1)} async-done(((bf16[8,2,32768]{2,1,0:T(2,128)(2,1)}), bf16[8,2,32768]{2,1,0:T(2,128)(2,1)}, u32[]{:S(2)}, u32[]{:S(2)}) %all-to-all-start.2) | async-done | bytes 1048608 | tf_op jit(solution)/shard_map/all_to_all | solution.py:229
  235.3 5.8 reshape.983
  245.8 25.9 %multiply_convert_fusion.1 = (bf16[2048,1024]{1,0:T(8,128)(2,1)}, f32[2048,1024]{1,0:T(8,128)}, f32[2048,1024]{1,0:T(8,128)}) fusion(f32[1024]{0:T(1024)S(1)} %convert_element_type.441, bf16[1024,1024]{1,0:T(8,128)(2,1)S(1)} %copy-done, bf16[2048,1,1024]{2,0,1:T(8,128)(2,1)} %all-gather.7.cloned.1.call-done), kind=kOutput, calls=%fused_computation.81 | convolution fusion | flops 4433379328 | bytes 27267072 | tf_op jit(solution)/shard_map/rsd,df->rsf/dot_general | solution.py:202
  271.7 7.7 all-gather.9.cloned.1.call-done
  279.4 13.9 %fusion.186 = (bf16[1024]{0:T(1024)(128)(2,1)}, bf16[2048,1024]{1,0:T(8,128)(2,1)S(1)}) fusion(f32[2048,1024]{1,0:T(8,128)} %get-tuple-element.358, bf16[1024,1024]{1,0:T(8,128)(2,1)} %param.30, bf16[2048,1,1024]{2,0,1:T(8,128)(2,1)} %all-gather.9.cloned.1.call-done, f32[2048,1024]{1,0:T(8,128)} %get-tuple-element.369, f32[1024]{0:T(1024)S(1)} %convert_element_type.441), kind=kOutput, calls=%fused_computation.215 | convolution fusion | flops 4328520704 | bytes 27269120 | tf_op jit(solution)/shard_map/rsd,fd->rsf/dot_general | solution.py:251
  295.3 6.1 convert_bitcast_fusion
  303.0 8.8 convert_bitcast_fusion.1
  312.4 33.6 %reduce-scatter.9.cloned.1.call-done = bf16[512,1,1024]{2,0,1:T(8,128)(2,1)} async-done(((bf16[2048,1,1024]{2,0,1:T(8,128)(2,1)}), bf16[512,1,1024]{2,0,1:T(8,128)(2,1)}) %reduce-scatter.9.cloned.1.call-update) | async-done | bytes 1048592 | tf_op jit(solution)/shard_map/reduce_scatter | solution.py:259
  348.0 45.0 %reduce-scatter.7.cloned.1.call-done = bf16[512,1,1024]{2,0,1:T(8,128)(2,1)} async-done(((bf16[2048,1,1024]{2,0,1:T(8,128)(2,1)}), bf16[512,1,1024]{2,0,1:T(8,128)(2,1)}) %reduce-scatter.7.cloned.1.call-update) | async-done | bytes 1048592 | tf_op jit(solution)/shard_map/reduce_scatter | solution.py:207
  393.0 4.6 fusion.141
  400.9 9.5 fusion.150
  410.4 5.8 fusion.147
  416.2 19.3 %all-gather.11.cloned.1.call-done = bf16[2048,1,1024]{2,0,1:T(8,128)(2,1)} async-done(((bf16[512,1,1024]{2,0,1:T(8,128)(2,1)}), bf16[2048,1,1024]{2,0,1:T(8,128)(2,1)}) %all-gather.11.cloned.1.call-update) | async-done | bytes 4194320 | tf_op jit(solution)/shard_map/all_gather | solution.py:272
  445.9 282.8 %while.28 = (s32[]{:T(128)}, f32[2048,4,64]{0,2,1:T(8,128)}, f32[2048,4,64]{0,2,1:T(8,128)}, bf16[4,512,4,64]{1,3,2,0:T(8,128)(2,1)}, bf16[4,512,4,64]{1,3,2,0:T...) while((s32[]{:T(128)}, f32[2048,4,64]{0,2,1:T(8,128)}, ...), condition=%wide.region_20.21_spmd.clone, body=%wide.region_18.20_spmd.clone.sunk | while | flops 2796560384 | bytes 275323104 | solution.py:112
  450.9 6.8 fusion.246
  457.7 8.1 fusion.243
  465.8 24.0 %fusion.247 = bf16[4,512,4,64]{1,3,2,0:T(8,128)(2,1)} fusion(bf16[4,512,4,64]{1,3,2,0:T(8,128)(2,1)} %get-tuple-element.537, s32[]{:T(128)S(6)} %copy.184, bf16[2048,4,64]{0,2,1:T(8,128)(2,1)S(1)} %get-tuple-element.554, f32[4,512,2048]{2,1,0:T(8,128)} %fusion.243, f32[4,512,2048]{2,1,0:T(8,128)} %copy-done.2, ...), kind=kOutput, calls=%fused_computation.42.clone.1 | convolution fusion | flops 583012352 | bytes 70795264 | tf_op jit(solution)/shard_map/while/body/eval_jaxpr/hqk,khd->qhd/dot_general | solution.py:100
  489.8 25.5 %fusion.245 = f32[2048,4,64]{0,2,1:T(8,128)} fusion(f32[4,512,2048]{2,1,0:T(8,128)} %fusion.243, f32[4,512,2048]{2,1,0:T(8,128)} %copy-done.2, f32[4,512]{1,0:T(4,128)S(1)} %dynamic-slice_bitcast_fusion.2, pred[512,2048]{1,0:T(8,128)(4,1)S(1)} %broadcast_compare_fusion.5, f32[2048,4,64]{0,2,1:T(8,128)} %get-tuple-element.535, pred[]{:T(512)S(6)} %compare.3, ...), kind=kOutput, calls=%fused_computation.39.clone.1 | convolution fusion | flops 584060928 | bytes 73678856 | tf_op jit(solution)/shard_map/while/body/eval_jaxpr/hqk,qhd->khd/dot_general | solution.py:103
  520.1 8.0 fusion.246
  528.1 8.1 fusion.243
  536.2 24.0 %fusion.247 = bf16[4,512,4,64]{1,3,2,0:T(8,128)(2,1)} fusion(bf16[4,512,4,64]{1,3,2,0:T(8,128)(2,1)} %get-tuple-element.537, s32[]{:T(128)S(6)} %copy.184, bf16[2048,4,64]{0,2,1:T(8,128)(2,1)S(1)} %get-tuple-element.554, f32[4,512,2048]{2,1,0:T(8,128)} %fusion.243, f32[4,512,2048]{2,1,0:T(8,128)} %copy-done.2, ...), kind=kOutput, calls=%fused_computation.42.clone.1 | convolution fusion | flops 583012352 | bytes 70795264 | tf_op jit(solution)/shard_map/while/body/eval_jaxpr/hqk,khd->qhd/dot_general | solution.py:100
  560.2 26.1 %fusion.245 = f32[2048,4,64]{0,2,1:T(8,128)} fusion(f32[4,512,2048]{2,1,0:T(8,128)} %fusion.243, f32[4,512,2048]{2,1,0:T(8,128)} %copy-done.2, f32[4,512]{1,0:T(4,128)S(1)} %dynamic-slice_bitcast_fusion.2, pred[512,2048]{1,0:T(8,128)(4,1)S(1)} %broadcast_compare_fusion.5, f32[2048,4,64]{0,2,1:T(8,128)} %get-tuple-element.535, pred[]{:T(512)S(6)} %compare.3, ...), kind=kOutput, calls=%fused_computation.39.clone.1 | convolution fusion | flops 584060928 | bytes 73678856 | tf_op jit(solution)/shard_map/while/body/eval_jaxpr/hqk,qhd->khd/dot_general | solution.py:103
  591.1 8.0 fusion.246
  599.1 8.1 fusion.243
  607.2 24.0 %fusion.247 = bf16[4,512,4,64]{1,3,2,0:T(8,128)(2,1)} fusion(bf16[4,512,4,64]{1,3,2,0:T(8,128)(2,1)} %get-tuple-element.537, s32[]{:T(128)S(6)} %copy.184, bf16[2048,4,64]{0,2,1:T(8,128)(2,1)S(1)} %get-tuple-element.554, f32[4,512,2048]{2,1,0:T(8,128)} %fusion.243, f32[4,512,2048]{2,1,0:T(8,128)} %copy-done.2, ...), kind=kOutput, calls=%fused_computation.42.clone.1 | convolution fusion | flops 583012352 | bytes 70795264 | tf_op jit(solution)/shard_map/while/body/eval_jaxpr/hqk,khd->qhd/dot_general | solution.py:100
  631.2 26.1 %fusion.245 = f32[2048,4,64]{0,2,1:T(8,128)} fusion(f32[4,512,2048]{2,1,0:T(8,128)} %fusion.243, f32[4,512,2048]{2,1,0:T(8,128)} %copy-done.2, f32[4,512]{1,0:T(4,128)S(1)} %dynamic-slice_bitcast_fusion.2, pred[512,2048]{1,0:T(8,128)(4,1)S(1)} %broadcast_compare_fusion.5, f32[2048,4,64]{0,2,1:T(8,128)} %get-tuple-element.535, pred[]{:T(512)S(6)} %compare.3, ...), kind=kOutput, calls=%fused_computation.39.clone.1 | convolution fusion | flops 584060928 | bytes 73678856 | tf_op jit(solution)/shard_map/while/body/eval_jaxpr/hqk,qhd->khd/dot_general | solution.py:103
  662.1 8.0 fusion.246
  670.1 8.1 fusion.243
  678.2 24.0 %fusion.247 = bf16[4,512,4,64]{1,3,2,0:T(8,128)(2,1)} fusion(bf16[4,512,4,64]{1,3,2,0:T(8,128)(2,1)} %get-tuple-element.537, s32[]{:T(128)S(6)} %copy.184, bf16[2048,4,64]{0,2,1:T(8,128)(2,1)S(1)} %get-tuple-element.554, f32[4,512,2048]{2,1,0:T(8,128)} %fusion.243, f32[4,512,2048]{2,1,0:T(8,128)} %copy-done.2, ...), kind=kOutput, calls=%fused_computation.42.clone.1 | convolution fusion | flops 583012352 | bytes 70795264 | tf_op jit(solution)/shard_map/while/body/eval_jaxpr/hqk,khd->qhd/dot_general | solution.py:100
  702.2 26.1 %fusion.245 = f32[2048,4,64]{0,2,1:T(8,128)} fusion(f32[4,512,2048]{2,1,0:T(8,128)} %fusion.243, f32[4,512,2048]{2,1,0:T(8,128)} %copy-done.2, f32[4,512]{1,0:T(4,128)S(1)} %dynamic-slice_bitcast_fusion.2, pred[512,2048]{1,0:T(8,128)(4,1)S(1)} %broadcast_compare_fusion.5, f32[2048,4,64]{0,2,1:T(8,128)} %get-tuple-element.535, pred[]{:T(512)S(6)} %compare.3, ...), kind=kOutput, calls=%fused_computation.39.clone.1 | convolution fusion | flops 584060928 | bytes 73678856 | tf_op jit(solution)/shard_map/while/body/eval_jaxpr/hqk,qhd->khd/dot_general | solution.py:103
  738.6 4.4 fusion.160
  743.0 4.7 fusion.154
  749.0 7.1 fusion.118
  757.3 6.8 fusion.131
  768.0 4.4 all-to-all-start.3
  776.3 9.2 reduce.38
  788.1 4.2 all-to-all-start.1
  796.2 8.0 reduce.37
  805.8 4.6 all-to-all-done.1
  814.3 5.8 reshape.989
  822.8 5.8 reshape.987
  833.6 7.9 fusion.135
  848.3 8.6 fusion.136
  858.6 103.7 %all-reduce.5.cloned.1.call-done = (bf16[1024,3,256]{2,0,1:T(8,128)(2,1)}, bf16[256,1024]{1,0:T(8,128)(2,1)}, bf16[1024,1024]{1,0:T(8,128)(2,1)}, bf16[1024,1024]{1,0:T(8,128)(2,1)}) async-done(((bf16[1024,3,256]{2,0,1:T(8,128)(2,1)}, bf16[256,1024]{1,0:T(8,128)(2,1)}, bf16[1024,1024]{1,0:T(8,128)(2,1)}, bf16[1024,1024]{1,0:T(8,128)(2,1)}), (bf16[1024,3,256]{2,0,1:T(8,128)(2,1)}, ...) | async-done | bytes 6291472 | tf_op jit(solution)/shard_map/psum | solution.py:334
  973.4 35.0 %reduce-scatter.11.cloned.1.call-done = bf16[512,1,1024]{2,0,1:T(8,128)(2,1)} async-done(((bf16[2048,1,1024]{2,0,1:T(8,128)(2,1)}), bf16[512,1,1024]{2,0,1:T(8,128)(2,1)}) %reduce-scatter.11.cloned.1.call-update) | async-done | bytes 1048592 | tf_op jit(solution)/shard_map/reduce_scatter | solution.py:309
  1014.0 37.5 %all-reduce.1 = (bf16[1024]{0:T(1024)(128)(2,1)S(1)}, bf16[1024]{0:T(1024)(128)(2,1)S(1)}, bf16[1024]{0:T(1024)(128)(2,1)S(1)}, bf16[1024]{0:T(1024)(128)(2,1)S(...) all-reduce(bf16[1024]{0:T(1024)(128)(2,1)S(1)} %copy-done.48, ...), channel_id=1, replica_groups=mesh['section'=2,'rows'=4,'heads'=4] {'section','rows'}, use_global_device_ids=true, to_apply=%region_30.31 | all-reduce | flops 7680 | bytes 30720 | tf_op jit(solution)/shard_map/psum | solution.py:337
  1059.4 10.9 %all-reduce = (f32[1024]{0:T(1024)}, f32[1024]{0:T(1024)}, f32[1024]{0:T(1024)}, f32[1024]{0:T(1024)}, f32[1024]{0:T(1024)}, /*index=5*/f32[1024]{0:T(1024)}) all-reduce(bf16[1024]{0:T(1024)(128)(2,1)S(1)} %get-tuple-element.338, ...), channel_id=1, replica_groups=mesh['section'=2,'rows'=4,'heads'=4] {'heads'}, use_global_device_ids=true, to_apply=%region_31.32 | all-reduce | flops 6144 | bytes 36864 | tf_op jit(solution)/shard_map/psum | solution.py:348
  (313 shorter events, 172.1 us)
Async XLA Ops:
  7.2 238.6 %copy-start = (bf16[1024,1024]{1,0:T(8,128)(2,1)S(1)}, bf16[1024,1024]{1,0:T(8,128)(2,1)}, u32[]{:S(2)}) copy-start(bf16[1024,1024]{1,0:T(8,128)(2,1)} %param.28) | copy-start | bytes 6291460
  7.2 8.0 copy-start.51
  7.2 8.2 copy-start.44
  7.2 45.3 %all-gather.5.cloned.1.call-start = ((), (), s32[]{:S(2)}) async-start(), calls=%async_computation.8 | async-start | bytes 5242880 | tf_op jit(solution)/shard_map/all_gather | solution.py:161
  8.8 7.4 copy-start.31
  11.8 4.5 copy-start.27
  15.1 169.1 %reduce-scatter.5.cloned.1.call-start = ((), (), s32[]{:S(2)}) async-start(), calls=%async_computation.9 | async-start | bytes 5242880 | tf_op jit(solution)/shard_map/reduce_scatter | solution.py:188
  16.1 36.4 %copy-start.34 = (s32[2,6]{0,1:T(8,128)}, s32[2,6]{0,1:T(8,128)S(1)}, u32[]{:S(2)}) copy-start(s32[2,6]{0,1:T(8,128)S(1)} %reduce_window_sum.11) | copy-start | bytes 148
  16.3 36.2 %copy-start.29 = (s32[2,2048]{1,0:T(2,128)}, s32[2,2048]{1,0:T(2,128)S(1)}, u32[]{:S(2)}) copy-start(s32[2,2048]{1,0:T(2,128)S(1)} %fusion.165) | copy-start | bytes 49156
  75.1 4.4 copy-start.8
  75.1 4.4 copy-start.17
  90.8 4.4 copy-start.8
  90.8 4.4 copy-start.17
  106.5 4.4 copy-start.8
  106.5 4.4 copy-start.17
  122.2 4.4 copy-start.8
  139.5 106.2 %all-gather.7.cloned.1.call-start = ((), (), s32[]{:S(2)}) async-start(), calls=%async_computation.10 | async-start | bytes 5242880 | tf_op jit(solution)/shard_map/all_gather | solution.py:200
  139.7 50.4 %copy-start.50 = (s32[2,1,6]{2,1,0:T(1,128)S(1)}, s32[2,1,6]{2,1,0:T(1,128)}, u32[]{:S(2)}) copy-start(s32[2,1,6]{2,1,0:T(1,128)} %param.23) | copy-start | bytes 148
  139.7 50.5 %copy-start.45 = (s32[2,1,6]{2,1,0:T(1,128)S(1)}, s32[2,1,6]{2,1,0:T(1,128)}, u32[]{:S(2)}) copy-start(s32[2,1,6]{2,1,0:T(1,128)} %param.22) | copy-start | bytes 148
  139.7 50.9 %copy-start.35 = (s32[2,6]{0,1:T(8,128)S(1)}, s32[2,6]{0,1:T(8,128)}, u32[]{:S(2)}) copy-start(s32[2,6]{0,1:T(8,128)} %copy-done.34) | copy-start | bytes 148
  139.7 50.9 %copy-start.37 = (s32[2,6]{0,1:T(8,128)S(1)}, s32[2,6]{0,1:T(8,128)}, u32[]{:S(2)}) copy-start(s32[2,6]{0,1:T(8,128)} %copy-done.36) | copy-start | bytes 148
  139.7 50.9 %copy-start.30 = (s32[2,2048]{1,0:T(2,128)S(1)}, s32[2,2048]{1,0:T(2,128)}, u32[]{:S(2)}) copy-start(s32[2,2048]{1,0:T(2,128)} %copy-done.29) | copy-start | bytes 49156
  191.5 7.9 copy-start.42
  205.4 30.0 %all-to-all-start.2 = ((bf16[8,2,32768]{2,1,0:T(2,128)(2,1)}), bf16[8,2,32768]{2,1,0:T(2,128)(2,1)}, u32[]{:S(2)}, u32[]{:S(2)}) async-start(bf16[8,2,32768]{2,1,0:T(2,128)(2,1)} %reshape.982), calls=%async_computation.4 | async-start | bytes 2097152 | tf_op jit(solution)/shard_map/all_to_all | solution.py:229
  209.6 69.8 %all-gather.9.cloned.1.call-start = ((), (), s32[]{:S(2)}) async-start(), calls=%async_computation.12 | async-start | bytes 5242880 | tf_op jit(solution)/shard_map/all_gather | solution.py:247
  212.9 32.9 %copy-start.55 = (bf16[1024]{0:T(1024)(128)(2,1)S(1)}, bf16[1024]{0:T(1024)(128)(2,1)}, u32[]{:S(2)}) copy-start(bf16[1024]{0:T(1024)(128)(2,1)} %param.29) | copy-start | bytes 6148
  245.7 100.4 %reduce-scatter.9.cloned.1.call-start = ((), (), s32[]{:S(2)}) async-start(), calls=%async_computation.13 | async-start | bytes 5242880 | tf_op jit(solution)/shard_map/reduce_scatter | solution.py:259
  301.4 91.6 %reduce-scatter.7.cloned.1.call-start = ((), (), s32[]{:S(2)}) async-start(), calls=%async_computation.11 | async-start | bytes 5242880 | tf_op jit(solution)/shard_map/reduce_scatter | solution.py:207
  311.7 34.3 %copy-start.4 = (bf16[1,512,1,1024]{3,1,2,0:T(8,128)(2,1)S(1)}, bf16[1,512,1,1024]{3,1,2,0:T(8,128)(2,1)}, u32[]{:S(2)}) copy-start(bf16[1,512,1,1024]{3,1,2,0:T(8,128)(2,1)} %param.21) | copy-start | bytes 3145732
  311.7 34.3 %copy-start.7 = (bf16[512,1,1024]{2,0,1:T(8,128)(2,1)S(1)}, bf16[512,1,1024]{2,0,1:T(8,128)(2,1)}, u32[]{:S(2)}) copy-start(bf16[512,1,1024]{2,0,1:T(8,128)(2,1)} %reduce-scatter.5.cloned.1.call-done) | copy-start | bytes 3145732
  311.8 123.7 %all-gather.11.cloned.1.call-start = ((), (), s32[]{:S(2)}) async-start(), calls=%async_computation.14 | async-start | bytes 5242880 | tf_op jit(solution)/shard_map/all_gather | solution.py:272
  393.0 4.6 copy-start.12
  393.0 4.6 copy-start.13
  400.8 561.5 %all-reduce.5.cloned.1.call-start = ((), (), s32[]{:S(2)}) async-start(), calls=%async_computation.16 | async-start | bytes 12582912 | tf_op jit(solution)/shard_map/psum | solution.py:334
  400.9 9.5 copy-start.59
  400.9 9.5 copy-start.65
  410.4 25.1 %copy-start.63 = (bf16[256,1024]{1,0:T(8,128)(2,1)S(1)}, bf16[256,1024]{1,0:T(8,128)(2,1)}, u32[]{:S(2)}) copy-start(bf16[256,1024]{1,0:T(8,128)(2,1)} %param.26) | copy-start | bytes 1572868
  439.0 7.0 copy-start.9
  450.9 6.8 copy-start.2
  520.1 8.1 copy-start.2
  591.1 8.1 copy-start.2
  662.1 8.1 copy-start.2
  738.6 4.4 copy-start.21
  738.6 4.4 copy-start.24
  738.6 4.4 copy-start.26
  738.6 4.4 copy-start.58
  747.8 260.6 %reduce-scatter.11.cloned.1.call-start = ((), (), s32[]{:S(2)}) async-start(), calls=%async_computation.15 | async-start | bytes 5242880 | tf_op jit(solution)/shard_map/reduce_scatter | solution.py:309
  764.1 8.3 copy-start.5
  768.0 20.1 %all-to-all-start.3 = ((bf16[8,2,32768]{2,1,0:T(2,128)(2,1)}), bf16[8,2,32768]{2,1,0:T(2,128)(2,1)}, u32[]{:S(2)}, u32[]{:S(2)}) async-start(bf16[8,2,32768]{2,1,0:T(2,128)(2,1)} %reshape.988), calls=%async_computation.7 | async-start | bytes 2097152 | tf_op jit(solution)/shard_map/all_to_all | solution.py:236
  776.3 16.0 %copy-start.16 = (bf16[512,1,1024]{2,0,1:T(8,128)(2,1)S(1)}, bf16[512,1,1024]{2,0,1:T(8,128)(2,1)}, u32[]{:S(2)}) copy-start(bf16[512,1,1024]{2,0,1:T(8,128)(2,1)} %get-tuple-element.365) | copy-start | bytes 3145732
  788.1 22.4 %all-to-all-start.1 = ((bf16[8,2,32768]{2,1,0:T(2,128)(2,1)}), bf16[8,2,32768]{2,1,0:T(2,128)(2,1)}, u32[]{:S(2)}, u32[]{:S(2)}) async-start(bf16[8,2,32768]{2,1,0:T(2,128)(2,1)} %reshape.986), calls=%async_computation.3 | async-start | bytes 2097152 | tf_op jit(solution)/shard_map/all_to_all | solution.py:220
  796.2 18.0 %copy-start.33 = (s32[2,2048]{1,0:T(2,128)S(1)}, s32[2,2048]{1,0:T(2,128)}, u32[]{:S(2)}) copy-start(s32[2,2048]{1,0:T(2,128)} %get-tuple-element.373) | copy-start | bytes 49156
  810.5 31.1 %all-to-all-start = ((bf16[8,2,32768]{2,1,0:T(2,128)(2,1)}), bf16[8,2,32768]{2,1,0:T(2,128)(2,1)S(1)}, u32[]{:S(2)}, u32[]{:S(2)}) async-start(bf16[8,2,32768]{2,1,0:T(2,128)(2,1)} %reshape.984), calls=%async_computation.2 | async-start | bytes 2097152 | tf_op jit(solution)/shard_map/all_to_all | solution.py:219
  962.3 5.6 copy-start.20
  970.4 37.9 %copy-start.28 = (f32[1024]{0:T(1024)S(1)}, f32[1024]{0:T(1024)}, u32[]{:S(2)}) copy-start(f32[1024]{0:T(1024)} %copy-done.27) | copy-start | bytes 12292
  970.4 37.9 %copy-start.32 = (f32[512]{0:T(512)S(1)}, f32[512]{0:T(512)}, u32[]{:S(2)}) copy-start(f32[512]{0:T(512)} %copy-done.31) | copy-start | bytes 6148
  970.4 39.7 %copy-start.41 = (f32[512]{0:T(512)S(1)}, f32[512]{0:T(512)}, u32[]{:S(2)}) copy-start(f32[512]{0:T(512)} %copy-done.40) | copy-start | bytes 6148
  970.5 41.1 %copy-start.39 = (f32[512]{0:T(512)S(1)}, f32[512]{0:T(512)}, u32[]{:S(2)}) copy-start(f32[512]{0:T(512)} %copy-done.38) | copy-start | bytes 6148
  973.4 40.6 %copy-start.46 = (bf16[1024]{0:T(1024)(128)(2,1)S(1)}, bf16[1024]{0:T(1024)(128)(2,1)}, u32[]{:S(2)}) copy-start(bf16[1024]{0:T(1024)(128)(2,1)} %get-tuple-element.288) | copy-start | bytes 6148
  973.4 40.6 %copy-start.47 = (bf16[1024]{0:T(1024)(128)(2,1)S(1)}, bf16[1024]{0:T(1024)(128)(2,1)}, u32[]{:S(2)}) copy-start(bf16[1024]{0:T(1024)(128)(2,1)} %get-tuple-element.352) | copy-start | bytes 6148
  973.4 40.6 %copy-start.48 = (bf16[1024]{0:T(1024)(128)(2,1)S(1)}, bf16[1024]{0:T(1024)(128)(2,1)}, u32[]{:S(2)}) copy-start(bf16[1024]{0:T(1024)(128)(2,1)} %get-tuple-element.354) | copy-start | bytes 6148
  973.4 40.6 %copy-start.49 = (bf16[1024]{0:T(1024)(128)(2,1)S(1)}, bf16[1024]{0:T(1024)(128)(2,1)}, u32[]{:S(2)}) copy-start(bf16[1024]{0:T(1024)(128)(2,1)} %get-tuple-element.366) | copy-start | bytes 6148
  973.4 40.6 %copy-start.57 = (bf16[1024]{0:T(1024)(128)(2,1)S(1)}, bf16[1024]{0:T(1024)(128)(2,1)}, u32[]{:S(2)}) copy-start(bf16[1024]{0:T(1024)(128)(2,1)} %get-tuple-element.370) | copy-start | bytes 6148
  1052.1 18.2 %copy-start.1 = (bf16[1024,1024]{1,0:T(8,128)(2,1)S(1)}, bf16[1024,1024]{1,0:T(8,128)(2,1)}, u32[]{:S(2)}) copy-start(bf16[1024,1024]{1,0:T(8,128)(2,1)} %param.28) | copy-start | bytes 6291460
  (30 other events, 70.8 us)
Sparse Core Ops, SparseCore 0:
  15.3 37.1 all-gather.4
  139.7 44.4 reduce-scatter.4
  190.2 44.9 all-gather.6
  245.8 33.5 all-gather.8
  301.5 44.4 reduce-scatter.8
  348.4 44.4 reduce-scatter.6
  401.0 34.4 all-gather.10
  747.9 214.4 all-reduce.4
  964.9 43.4 reduce-scatter.10
where the time goes:
time: 1090 us; the launch traced here: 1080 us
  matrix products  445 us (41%)
  waiting for transfers between devices  351 us (32%)
  other arithmetic  104 us (10%)
  local copies, waits for them, and re-layouts  95.7 us (9%)
  blocking collectives  48.4 us (4%)
  starting transfers between devices  17.1 us (2%)
  between operations  15 us (1%)
    psum x1, waiting for transfers between devices, per_device(): lax.psum(grad_w_qkv_part.astype(jnp.bfloat16), ('section', 'rows'))  104 us
    dot_general x4, matrix products, one_block(): jnp.einsum('hqk,qhd->khd', grad_score, queries, preferred_element_type=jn...  104 us
    dot_general x4, matrix products, one_block(): jnp.einsum('hqk,khd->qhd', grad_score, key_seq, preferred_element_type=jn...  96 us
    unnamed x136, local copies, waits for them, and re-layouts  51.9 us
    reduce_scatter x1, waiting for transfers between devices, per_device(): lax.psum_scatter(jnp.einsum('rsf,fd->rsd', picked, w_down, preferred_elem...  45 us
    reduce_scatter x1, waiting for transfers between devices, per_device(): lax.psum_scatter(jnp.einsum('rsk,kd->rsd', picked, w_out, preferred_eleme...  44.5 us
    psum x1, blocking collectives, per_device(): lax.psum(grad_b_out.astype(jnp.bfloat16), ('section', 'rows'))  37.5 us
    all_gather x1, waiting for transfers between devices, per_device(): gathered_one = lax.all_gather(normed_one, 'heads', axis=0, tiled=True)  35 us
  transfers between devices with their start and end apart: 13, of which 10 were waited for; matrix products, arithmetic and copies ran while one was open for 17% of the time, Pallas kernels for 0%

commit v1 on v0

--- a/solution.py
+++ b/solution.py
@@ -317,6 +317,9 @@
     norm_one_back = jax.vjp(layer_norm, token_values, ln1_gain, ln1_bias)[1]
     grad_input, grad_gain_one, grad_shift_one = norm_one_back(grad_normed_one)
     grad_tokens = grad_input + grad_after + grad_direct.astype(jnp.float32)
+    domain_number = lambda incoming_x: jnp.sum(
+        lax.all_gather(incoming_x, ("section", "rows")), axis=0
+    )
     (
         grad_w_qkv_part,
         grad_b_qv,
@@ -334,7 +337,7 @@
         lax.psum(grad_w_qkv_part.astype(jnp.bfloat16), ("section", "rows")).astype(jnp.float32),
         lax.psum(grad_b_qv.astype(jnp.bfloat16), ("section", "rows")).astype(jnp.float32),
         lax.psum(grad_w_out_part.astype(jnp.bfloat16), ("section", "rows")).astype(jnp.float32),
-        lax.psum(grad_b_out.astype(jnp.bfloat16), ("section", "rows")).astype(jnp.float32),
+        domain_number(grad_b_out.astype(jnp.bfloat16)).astype(jnp.float32),
         lax.psum(grad_gain_one, ("section", "rows")).astype(jnp.float32),
         lax.psum(grad_shift_one, ("section", "rows")).astype(jnp.float32),
         lax.psum(grad_w_up_part.astype(jnp.bfloat16), ("section", "rows")).astype(jnp.float32),

time: 1090 us -> 1090 us (level)
  blocking collectives: 48.4 us -> 75.8 us
  waiting for transfers between devices: 351 us -> 324 us
    all_gather x0 -> x1, blocking collectives: none -> 27.6 us  [per_device(): lax.all_gather(incoming_x, ('section', 'rows'))]
    psum x1, waiting for transfers between devices: 104 us -> 76.6 us  [per_device(): lax.psum(grad_w_qkv_part.astype(jnp.bfloat16), ('section', 'rows'))]
where the time goes in v1:
time: 1090 us; the launch traced here: 1080 us
  matrix products  445 us (41%)
  waiting for transfers between devices  324 us (30%)
  other arithmetic  104 us (10%)
  local copies, waits for them, and re-layouts  95.8 us (9%)
  blocking collectives  75.8 us (7%)
  starting transfers between devices  16.8 us (2%)
  between operations  14.8 us (1%)
    dot_general x4, matrix products, one_block(): jnp.einsum('hqk,qhd->khd', grad_score, queries, preferred_element_type=jn...  104 us
    dot_general x4, matrix products, one_block(): jnp.einsum('hqk,khd->qhd', grad_score, key_seq, preferred_element_type=jn...  96 us
    psum x1, waiting for transfers between devices, per_device(): lax.psum(grad_w_qkv_part.astype(jnp.bfloat16), ('section', 'rows'))  76.6 us
    unnamed x136, local copies, waits for them, and re-layouts  52.1 us
    reduce_scatter x1, waiting for transfers between devices, per_device(): lax.psum_scatter(jnp.einsum('rsf,fd->rsd', picked, w_down, preferred_elem...  44.9 us
    reduce_scatter x1, waiting for transfers between devices, per_device(): lax.psum_scatter(jnp.einsum('rsk,kd->rsd', picked, w_out, preferred_eleme...  44.5 us
    psum x1, blocking collectives, per_device(): lax.psum(grad_b_down.astype(jnp.bfloat16), ('section', 'rows'))  37.3 us
    all_gather x1, waiting for transfers between devices, per_device(): gathered_one = lax.all_gather(normed_one, 'heads', axis=0, tiled=True)  35 us
  transfers between devices with their start and end apart: 13, of which 10 were waited for; matrix products, arithmetic and copies ran while one was open for 17% of the time, Pallas kernels for 0%

profile of v1, /device:TPU:0, one launch (start us, length us, event | category | flops | bytes accessed | tf_op | source)
XLA Modules:
  0.0 1077.4 jit_solution(12064455370518345605)
XLA Ops:
  17.5 35.0 %all-gather.6.cloned.1.call-done = bf16[2048,1,1024]{2,0,1:T(8,128)(2,1)} async-done(((bf16[512,1,1024]{2,0,1:T(8,128)(2,1)}), bf16[2048,1,1024]{2,0,1:T(8,128)(2,1)}) %all-gather.6.cloned.1.call-update) | async-done | bytes 4194320 | tf_op jit(solution)/shard_map/all_gather | solution.py:161
  52.5 5.8 fusion.115
  69.9 63.2 %while.27 = (s32[]{:T(128)}, bf16[4,512,4,64]{1,3,2,0:T(8,128)(2,1)}, f32[4,4,512]{2,1,0:T(4,128)}, s32[4,512]{1,0:T(4,128)S(1)}, s32[1,2048]{1,0:T(1,128)S(1)},...) while((s32[]{:T(128)}, ...), condition=%wide.region_7.8_spmd, body=%wide.region_4.7_spmd.sunk | while | flops 1125120000 | bytes 70072528 | solution.py:78
  70.6 4.5 fusion.230
  75.1 4.4 fusion.231
  79.6 5.1 fusion.232
  86.3 4.5 fusion.230
  90.8 4.4 fusion.231
  95.3 5.1 fusion.232
  102.0 4.5 fusion.230
  106.5 4.4 fusion.231
  110.9 5.1 fusion.232
  117.7 4.5 fusion.230
  122.2 4.4 fusion.231
  126.6 5.1 fusion.232
  140.0 44.5 %reduce-scatter.5.cloned.1.call-done = bf16[512,1,1024]{2,0,1:T(8,128)(2,1)} async-done(((bf16[2048,1,1024]{2,0,1:T(8,128)(2,1)}), bf16[512,1,1024]{2,0,1:T(8,128)(2,1)}) %reduce-scatter.5.cloned.1.call-update) | async-done | bytes 1048592 | tf_op jit(solution)/shard_map/reduce_scatter | solution.py:188
  191.8 7.9 fusion.130
  213.0 22.6 %all-to-all-done.2 = bf16[8,2,32768]{2,1,0:T(2,128)(2,1)} async-done(((bf16[8,2,32768]{2,1,0:T(2,128)(2,1)}), bf16[8,2,32768]{2,1,0:T(2,128)(2,1)}, u32[]{:S(2)}, u32[]{:S(2)}) %all-to-all-start.2) | async-done | bytes 1048608 | tf_op jit(solution)/shard_map/all_to_all | solution.py:229
  235.6 5.8 reshape.984
  246.1 25.8 %multiply_convert_fusion.1 = (bf16[2048,1024]{1,0:T(8,128)(2,1)}, f32[2048,1024]{1,0:T(8,128)}, f32[2048,1024]{1,0:T(8,128)}) fusion(f32[1024]{0:T(1024)S(1)} %convert_element_type.443, bf16[1024,1024]{1,0:T(8,128)(2,1)S(1)} %copy-done, bf16[2048,1,1024]{2,0,1:T(8,128)(2,1)} %all-gather.8.cloned.1.call-done), kind=kOutput, calls=%fused_computation.81 | convolution fusion | flops 4433379328 | bytes 27267072 | tf_op jit(solution)/shard_map/rsd,df->rsf/dot_general | solution.py:202
  271.9 7.8 all-gather.10.cloned.1.call-done
  279.7 13.9 %fusion.186 = (bf16[1024]{0:T(1024)(128)(2,1)}, bf16[2048,1024]{1,0:T(8,128)(2,1)S(1)}) fusion(f32[2048,1024]{1,0:T(8,128)} %get-tuple-element.357, bf16[1024,1024]{1,0:T(8,128)(2,1)} %param.30, bf16[2048,1,1024]{2,0,1:T(8,128)(2,1)} %all-gather.10.cloned.1.call-done, f32[2048,1024]{1,0:T(8,128)} %get-tuple-element.368, f32[1024]{0:T(1024)S(1)} %convert_element_type.443), kind=kOutput, calls=%fused_computation.215 | convolution fusion | flops 4328520704 | bytes 27269120 | tf_op jit(solution)/shard_map/rsd,fd->rsf/dot_general | solution.py:251
  295.6 6.1 convert_bitcast_fusion
  303.2 8.7 convert_bitcast_fusion.1
  312.6 33.7 %reduce-scatter.9.cloned.1.call-done = bf16[512,1,1024]{2,0,1:T(8,128)(2,1)} async-done(((bf16[2048,1,1024]{2,0,1:T(8,128)(2,1)}), bf16[512,1,1024]{2,0,1:T(8,128)(2,1)}) %reduce-scatter.9.cloned.1.call-update) | async-done | bytes 1048592 | tf_op jit(solution)/shard_map/reduce_scatter | solution.py:259
  348.3 44.9 %reduce-scatter.7.cloned.1.call-done = bf16[512,1,1024]{2,0,1:T(8,128)(2,1)} async-done(((bf16[2048,1,1024]{2,0,1:T(8,128)(2,1)}), bf16[512,1,1024]{2,0,1:T(8,128)(2,1)}) %reduce-scatter.7.cloned.1.call-update) | async-done | bytes 1048592 | tf_op jit(solution)/shard_map/reduce_scatter | solution.py:207
  393.3 4.6 fusion.141
  401.2 9.5 fusion.150
  410.7 5.8 fusion.147
  416.5 19.3 %all-gather.12.cloned.1.call-done = bf16[2048,1,1024]{2,0,1:T(8,128)(2,1)} async-done(((bf16[512,1,1024]{2,0,1:T(8,128)(2,1)}), bf16[2048,1,1024]{2,0,1:T(8,128)(2,1)}) %all-gather.12.cloned.1.call-update) | async-done | bytes 4194320 | tf_op jit(solution)/shard_map/all_gather | solution.py:272
  446.2 282.8 %while.28 = (s32[]{:T(128)}, f32[2048,4,64]{0,2,1:T(8,128)}, f32[2048,4,64]{0,2,1:T(8,128)}, bf16[4,512,4,64]{1,3,2,0:T(8,128)(2,1)}, bf16[4,512,4,64]{1,3,2,0:T...) while((s32[]{:T(128)}, f32[2048,4,64]{0,2,1:T(8,128)}, ...), condition=%wide.region_20.21_spmd.clone, body=%wide.region_18.20_spmd.clone.sunk | while | flops 2796560384 | bytes 275323104 | solution.py:112
  451.2 6.8 fusion.246
  458.0 8.1 fusion.243
  466.1 24.0 %fusion.247 = bf16[4,512,4,64]{1,3,2,0:T(8,128)(2,1)} fusion(bf16[4,512,4,64]{1,3,2,0:T(8,128)(2,1)} %get-tuple-element.536, s32[]{:T(128)S(6)} %copy.184, bf16[2048,4,64]{0,2,1:T(8,128)(2,1)S(1)} %get-tuple-element.553, f32[4,512,2048]{2,1,0:T(8,128)} %fusion.243, f32[4,512,2048]{2,1,0:T(8,128)} %copy-done.2, ...), kind=kOutput, calls=%fused_computation.42.clone.1 | convolution fusion | flops 583012352 | bytes 70795264 | tf_op jit(solution)/shard_map/while/body/eval_jaxpr/hqk,khd->qhd/dot_general | solution.py:100
  490.1 25.5 %fusion.245 = f32[2048,4,64]{0,2,1:T(8,128)} fusion(f32[4,512,2048]{2,1,0:T(8,128)} %fusion.243, f32[4,512,2048]{2,1,0:T(8,128)} %copy-done.2, f32[4,512]{1,0:T(4,128)S(1)} %dynamic-slice_bitcast_fusion.2, pred[512,2048]{1,0:T(8,128)(4,1)S(1)} %broadcast_compare_fusion.5, f32[2048,4,64]{0,2,1:T(8,128)} %get-tuple-element.534, pred[]{:T(512)S(6)} %compare.3, ...), kind=kOutput, calls=%fused_computation.39.clone.1 | convolution fusion | flops 584060928 | bytes 73678856 | tf_op jit(solution)/shard_map/while/body/eval_jaxpr/hqk,qhd->khd/dot_general | solution.py:103
  520.4 8.0 fusion.246
  528.4 8.1 fusion.243
  536.5 24.0 %fusion.247 = bf16[4,512,4,64]{1,3,2,0:T(8,128)(2,1)} fusion(bf16[4,512,4,64]{1,3,2,0:T(8,128)(2,1)} %get-tuple-element.536, s32[]{:T(128)S(6)} %copy.184, bf16[2048,4,64]{0,2,1:T(8,128)(2,1)S(1)} %get-tuple-element.553, f32[4,512,2048]{2,1,0:T(8,128)} %fusion.243, f32[4,512,2048]{2,1,0:T(8,128)} %copy-done.2, ...), kind=kOutput, calls=%fused_computation.42.clone.1 | convolution fusion | flops 583012352 | bytes 70795264 | tf_op jit(solution)/shard_map/while/body/eval_jaxpr/hqk,khd->qhd/dot_general | solution.py:100
  560.5 26.1 %fusion.245 = f32[2048,4,64]{0,2,1:T(8,128)} fusion(f32[4,512,2048]{2,1,0:T(8,128)} %fusion.243, f32[4,512,2048]{2,1,0:T(8,128)} %copy-done.2, f32[4,512]{1,0:T(4,128)S(1)} %dynamic-slice_bitcast_fusion.2, pred[512,2048]{1,0:T(8,128)(4,1)S(1)} %broadcast_compare_fusion.5, f32[2048,4,64]{0,2,1:T(8,128)} %get-tuple-element.534, pred[]{:T(512)S(6)} %compare.3, ...), kind=kOutput, calls=%fused_computation.39.clone.1 | convolution fusion | flops 584060928 | bytes 73678856 | tf_op jit(solution)/shard_map/while/body/eval_jaxpr/hqk,qhd->khd/dot_general | solution.py:103
  591.4 8.0 fusion.246
  599.5 8.1 fusion.243
  607.6 24.0 %fusion.247 = bf16[4,512,4,64]{1,3,2,0:T(8,128)(2,1)} fusion(bf16[4,512,4,64]{1,3,2,0:T(8,128)(2,1)} %get-tuple-element.536, s32[]{:T(128)S(6)} %copy.184, bf16[2048,4,64]{0,2,1:T(8,128)(2,1)S(1)} %get-tuple-element.553, f32[4,512,2048]{2,1,0:T(8,128)} %fusion.243, f32[4,512,2048]{2,1,0:T(8,128)} %copy-done.2, ...), kind=kOutput, calls=%fused_computation.42.clone.1 | convolution fusion | flops 583012352 | bytes 70795264 | tf_op jit(solution)/shard_map/while/body/eval_jaxpr/hqk,khd->qhd/dot_general | solution.py:100
  631.6 26.1 %fusion.245 = f32[2048,4,64]{0,2,1:T(8,128)} fusion(f32[4,512,2048]{2,1,0:T(8,128)} %fusion.243, f32[4,512,2048]{2,1,0:T(8,128)} %copy-done.2, f32[4,512]{1,0:T(4,128)S(1)} %dynamic-slice_bitcast_fusion.2, pred[512,2048]{1,0:T(8,128)(4,1)S(1)} %broadcast_compare_fusion.5, f32[2048,4,64]{0,2,1:T(8,128)} %get-tuple-element.534, pred[]{:T(512)S(6)} %compare.3, ...), kind=kOutput, calls=%fused_computation.39.clone.1 | convolution fusion | flops 584060928 | bytes 73678856 | tf_op jit(solution)/shard_map/while/body/eval_jaxpr/hqk,qhd->khd/dot_general | solution.py:103
  662.4 8.0 fusion.246
  670.5 8.1 fusion.243
  678.6 24.0 %fusion.247 = bf16[4,512,4,64]{1,3,2,0:T(8,128)(2,1)} fusion(bf16[4,512,4,64]{1,3,2,0:T(8,128)(2,1)} %get-tuple-element.536, s32[]{:T(128)S(6)} %copy.184, bf16[2048,4,64]{0,2,1:T(8,128)(2,1)S(1)} %get-tuple-element.553, f32[4,512,2048]{2,1,0:T(8,128)} %fusion.243, f32[4,512,2048]{2,1,0:T(8,128)} %copy-done.2, ...), kind=kOutput, calls=%fused_computation.42.clone.1 | convolution fusion | flops 583012352 | bytes 70795264 | tf_op jit(solution)/shard_map/while/body/eval_jaxpr/hqk,khd->qhd/dot_general | solution.py:100
  702.6 26.1 %fusion.245 = f32[2048,4,64]{0,2,1:T(8,128)} fusion(f32[4,512,2048]{2,1,0:T(8,128)} %fusion.243, f32[4,512,2048]{2,1,0:T(8,128)} %copy-done.2, f32[4,512]{1,0:T(4,128)S(1)} %dynamic-slice_bitcast_fusion.2, pred[512,2048]{1,0:T(8,128)(4,1)S(1)} %broadcast_compare_fusion.5, f32[2048,4,64]{0,2,1:T(8,128)} %get-tuple-element.534, pred[]{:T(512)S(6)} %compare.3, ...), kind=kOutput, calls=%fused_computation.39.clone.1 | convolution fusion | flops 584060928 | bytes 73678856 | tf_op jit(solution)/shard_map/while/body/eval_jaxpr/hqk,qhd->khd/dot_general | solution.py:103
  738.9 4.4 fusion.160
  743.4 4.7 fusion.154
  749.3 7.1 fusion.118
  757.7 6.7 fusion.131
  776.4 9.1 reduce.39
  788.0 4.4 all-to-all-start.1
  796.4 8.0 reduce.38
  805.9 4.7 all-to-all-done.1
  814.2 5.8 reshape.990
  822.7 5.8 reshape.988
  833.6 7.9 fusion.135
  841.5 27.6 %all-gather = bf16[8192]{0:T(1024)(128)(2,1)S(1)} all-gather(bf16[1024]{0:T(1024)(128)(2,1)S(1)} %copy-done.48), channel_id=2, replica_groups=mesh['section'=2,'rows'=4,'heads'=4] {'section','rows'}, dimensions={0}, use_global_device_ids=true | all-gather | bytes 18432 | tf_op jit(solution)/shard_map/all_gather | solution.py:321
  876.0 8.6 fusion.136
  886.4 76.6 %all-reduce.5.cloned.1.call-done = (bf16[1024,3,256]{2,0,1:T(8,128)(2,1)}, bf16[256,1024]{1,0:T(8,128)(2,1)}, bf16[1024,1024]{1,0:T(8,128)(2,1)}, bf16[1024,1024]{1,0:T(8,128)(2,1)}) async-done(((bf16[1024,3,256]{2,0,1:T(8,128)(2,1)}, bf16[256,1024]{1,0:T(8,128)(2,1)}, bf16[1024,1024]{1,0:T(8,128)(2,1)}, bf16[1024,1024]{1,0:T(8,128)(2,1)}), (bf16[1024,3,256]{2,0,1:T(8,128)(2,1)}, ...) | async-done | bytes 6291472 | tf_op jit(solution)/shard_map/psum | solution.py:337
  974.0 35.0 %reduce-scatter.11.cloned.1.call-done = bf16[512,1,1024]{2,0,1:T(8,128)(2,1)} async-done(((bf16[2048,1,1024]{2,0,1:T(8,128)(2,1)}), bf16[512,1,1024]{2,0,1:T(8,128)(2,1)}) %reduce-scatter.11.cloned.1.call-update) | async-done | bytes 1048592 | tf_op jit(solution)/shard_map/reduce_scatter | solution.py:309
  1014.6 37.3 %all-reduce.1 = (bf16[1024]{0:T(1024)(128)(2,1)S(1)}, bf16[1024]{0:T(1024)(128)(2,1)S(1)}, bf16[1024]{0:T(1024)(128)(2,1)S(1)}, bf16[1024]{0:T(1024)(128)(2,1)S(...) all-reduce(bf16[1024]{0:T(1024)(128)(2,1)S(1)} %copy-done.47, ...), channel_id=1, replica_groups=mesh['section'=2,'rows'=4,'heads'=4] {'section','rows'}, use_global_device_ids=true, to_apply=%region_37.38 | all-reduce | flops 6656 | bytes 26624 | tf_op jit(solution)/shard_map/psum | solution.py:346
  1059.7 10.9 %all-reduce = (f32[1024]{0:T(1024)}, f32[1024]{0:T(1024)}, f32[1024]{0:T(1024)}, f32[1024]{0:T(1024)}, f32[1024]{0:T(1024)}, /*index=5*/f32[1024]{0:T(1024)}) all-reduce(bf16[1024]{0:T(1024)(128)(2,1)S(1)} %reduce_sum.300, bf16[1024]{0:T(1024)(128)(2,1)S(1)} %get-tuple-element.338, ...), channel_id=1, replica_groups=mesh['section'=2,'rows'=4,'heads'=4] {'heads'}, use_global_device_ids=true, to_apply=%region_31.32 | all-reduce | flops 6144 | bytes 36864 | tf_op jit(solution)/shard_map/psum | solution.py:351
  (316 shorter events, 176.1 us)
Async XLA Ops:
  7.2 238.9 %copy-start = (bf16[1024,1024]{1,0:T(8,128)(2,1)S(1)}, bf16[1024,1024]{1,0:T(8,128)(2,1)}, u32[]{:S(2)}) copy-start(bf16[1024,1024]{1,0:T(8,128)(2,1)} %param.28) | copy-start | bytes 6291460
  7.2 8.0 copy-start.51
  7.2 8.2 copy-start.44
  7.2 45.2 %all-gather.6.cloned.1.call-start = ((), (), s32[]{:S(2)}) async-start(), calls=%async_computation.8 | async-start | bytes 5242880 | tf_op jit(solution)/shard_map/all_gather | solution.py:161
  8.8 7.4 copy-start.31
  11.8 4.5 copy-start.27
  15.1 169.4 %reduce-scatter.5.cloned.1.call-start = ((), (), s32[]{:S(2)}) async-start(), calls=%async_computation.9 | async-start | bytes 5242880 | tf_op jit(solution)/shard_map/reduce_scatter | solution.py:188
  16.1 36.4 %copy-start.34 = (s32[2,6]{0,1:T(8,128)}, s32[2,6]{0,1:T(8,128)S(1)}, u32[]{:S(2)}) copy-start(s32[2,6]{0,1:T(8,128)S(1)} %reduce_window_sum.11) | copy-start | bytes 148
  16.2 36.2 %copy-start.29 = (s32[2,2048]{1,0:T(2,128)}, s32[2,2048]{1,0:T(2,128)S(1)}, u32[]{:S(2)}) copy-start(s32[2,2048]{1,0:T(2,128)S(1)} %fusion.165) | copy-start | bytes 49156
  75.1 4.4 copy-start.8
  75.1 4.4 copy-start.17
  90.8 4.4 copy-start.8
  90.8 4.4 copy-start.17
  106.5 4.4 copy-start.8
  106.5 4.4 copy-start.17
  122.2 4.4 copy-start.8
  139.8 106.2 %all-gather.8.cloned.1.call-start = ((), (), s32[]{:S(2)}) async-start(), calls=%async_computation.10 | async-start | bytes 5242880 | tf_op jit(solution)/shard_map/all_gather | solution.py:200
  139.9 50.4 %copy-start.50 = (s32[2,1,6]{2,1,0:T(1,128)S(1)}, s32[2,1,6]{2,1,0:T(1,128)}, u32[]{:S(2)}) copy-start(s32[2,1,6]{2,1,0:T(1,128)} %param.23) | copy-start | bytes 148
  140.0 50.5 %copy-start.45 = (s32[2,1,6]{2,1,0:T(1,128)S(1)}, s32[2,1,6]{2,1,0:T(1,128)}, u32[]{:S(2)}) copy-start(s32[2,1,6]{2,1,0:T(1,128)} %param.22) | copy-start | bytes 148
  140.0 50.9 %copy-start.35 = (s32[2,6]{0,1:T(8,128)S(1)}, s32[2,6]{0,1:T(8,128)}, u32[]{:S(2)}) copy-start(s32[2,6]{0,1:T(8,128)} %copy-done.34) | copy-start | bytes 148
  140.0 50.9 %copy-start.37 = (s32[2,6]{0,1:T(8,128)S(1)}, s32[2,6]{0,1:T(8,128)}, u32[]{:S(2)}) copy-start(s32[2,6]{0,1:T(8,128)} %copy-done.36) | copy-start | bytes 148
  140.0 50.9 %copy-start.30 = (s32[2,2048]{1,0:T(2,128)S(1)}, s32[2,2048]{1,0:T(2,128)}, u32[]{:S(2)}) copy-start(s32[2,2048]{1,0:T(2,128)} %copy-done.29) | copy-start | bytes 49156
  191.8 7.9 copy-start.42
  205.5 30.1 %all-to-all-start.2 = ((bf16[8,2,32768]{2,1,0:T(2,128)(2,1)}), bf16[8,2,32768]{2,1,0:T(2,128)(2,1)}, u32[]{:S(2)}, u32[]{:S(2)}) async-start(bf16[8,2,32768]{2,1,0:T(2,128)(2,1)} %reshape.983), calls=%async_computation.4 | async-start | bytes 2097152 | tf_op jit(solution)/shard_map/all_to_all | solution.py:229
  209.8 69.9 %all-gather.10.cloned.1.call-start = ((), (), s32[]{:S(2)}) async-start(), calls=%async_computation.12 | async-start | bytes 5242880 | tf_op jit(solution)/shard_map/all_gather | solution.py:247
  213.0 33.0 %copy-start.55 = (bf16[1024]{0:T(1024)(128)(2,1)S(1)}, bf16[1024]{0:T(1024)(128)(2,1)}, u32[]{:S(2)}) copy-start(bf16[1024]{0:T(1024)(128)(2,1)} %param.29) | copy-start | bytes 6148
  246.0 100.4 %reduce-scatter.9.cloned.1.call-start = ((), (), s32[]{:S(2)}) async-start(), calls=%async_computation.13 | async-start | bytes 5242880 | tf_op jit(solution)/shard_map/reduce_scatter | solution.py:259
  301.7 91.6 %reduce-scatter.7.cloned.1.call-start = ((), (), s32[]{:S(2)}) async-start(), calls=%async_computation.11 | async-start | bytes 5242880 | tf_op jit(solution)/shard_map/reduce_scatter | solution.py:207
  312.0 34.4 %copy-start.4 = (bf16[1,512,1,1024]{3,1,2,0:T(8,128)(2,1)S(1)}, bf16[1,512,1,1024]{3,1,2,0:T(8,128)(2,1)}, u32[]{:S(2)}) copy-start(bf16[1,512,1,1024]{3,1,2,0:T(8,128)(2,1)} %param.21) | copy-start | bytes 3145732
  312.0 34.4 %copy-start.7 = (bf16[512,1,1024]{2,0,1:T(8,128)(2,1)S(1)}, bf16[512,1,1024]{2,0,1:T(8,128)(2,1)}, u32[]{:S(2)}) copy-start(bf16[512,1,1024]{2,0,1:T(8,128)(2,1)} %reduce-scatter.5.cloned.1.call-done) | copy-start | bytes 3145732
  312.0 123.8 %all-gather.12.cloned.1.call-start = ((), (), s32[]{:S(2)}) async-start(), calls=%async_computation.14 | async-start | bytes 5242880 | tf_op jit(solution)/shard_map/all_gather | solution.py:272
  393.2 4.6 copy-start.12
  393.3 4.6 copy-start.13
  401.1 561.8 %all-reduce.5.cloned.1.call-start = ((), (), s32[]{:S(2)}) async-start(), calls=%async_computation.16 | async-start | bytes 12582912 | tf_op jit(solution)/shard_map/psum | solution.py:337
  401.2 9.5 copy-start.59
  401.2 9.5 copy-start.65
  410.7 25.1 %copy-start.63 = (bf16[256,1024]{1,0:T(8,128)(2,1)S(1)}, bf16[256,1024]{1,0:T(8,128)(2,1)}, u32[]{:S(2)}) copy-start(bf16[256,1024]{1,0:T(8,128)(2,1)} %param.26) | copy-start | bytes 1572868
  439.3 6.9 copy-start.9
  451.2 6.8 copy-start.2
  520.4 8.1 copy-start.2
  591.4 8.1 copy-start.2
  662.4 8.1 copy-start.2
  738.9 4.5 copy-start.21
  738.9 4.5 copy-start.24
  738.9 4.5 copy-start.26
  738.9 4.5 copy-start.58
  748.1 260.9 %reduce-scatter.11.cloned.1.call-start = ((), (), s32[]{:S(2)}) async-start(), calls=%async_computation.15 | async-start | bytes 5242880 | tf_op jit(solution)/shard_map/reduce_scatter | solution.py:309
  764.4 8.1 copy-start.5
  768.2 19.8 %all-to-all-start.3 = ((bf16[8,2,32768]{2,1,0:T(2,128)(2,1)}), bf16[8,2,32768]{2,1,0:T(2,128)(2,1)}, u32[]{:S(2)}, u32[]{:S(2)}) async-start(bf16[8,2,32768]{2,1,0:T(2,128)(2,1)} %reshape.989), calls=%async_computation.7 | async-start | bytes 2097152 | tf_op jit(solution)/shard_map/all_to_all | solution.py:236
  776.4 16.1 %copy-start.16 = (bf16[512,1,1024]{2,0,1:T(8,128)(2,1)S(1)}, bf16[512,1,1024]{2,0,1:T(8,128)(2,1)}, u32[]{:S(2)}) copy-start(bf16[512,1,1024]{2,0,1:T(8,128)(2,1)} %get-tuple-element.364) | copy-start | bytes 3145732
  788.0 22.6 %all-to-all-start.1 = ((bf16[8,2,32768]{2,1,0:T(2,128)(2,1)}), bf16[8,2,32768]{2,1,0:T(2,128)(2,1)}, u32[]{:S(2)}, u32[]{:S(2)}) async-start(bf16[8,2,32768]{2,1,0:T(2,128)(2,1)} %reshape.987), calls=%async_computation.3 | async-start | bytes 2097152 | tf_op jit(solution)/shard_map/all_to_all | solution.py:220
  796.4 17.8 %copy-start.33 = (s32[2,2048]{1,0:T(2,128)S(1)}, s32[2,2048]{1,0:T(2,128)}, u32[]{:S(2)}) copy-start(s32[2,2048]{1,0:T(2,128)} %get-tuple-element.372) | copy-start | bytes 49156
  810.6 58.5 %all-to-all-start = ((bf16[8,2,32768]{2,1,0:T(2,128)(2,1)}), bf16[8,2,32768]{2,1,0:T(2,128)(2,1)S(1)}, u32[]{:S(2)}, u32[]{:S(2)}) async-start(bf16[8,2,32768]{2,1,0:T(2,128)(2,1)} %reshape.985), calls=%async_computation.2 | async-start | bytes 2097152 | tf_op jit(solution)/shard_map/all_to_all | solution.py:219
  833.6 7.9 copy-start.48
  963.0 5.6 copy-start.20
  971.1 37.9 %copy-start.28 = (f32[1024]{0:T(1024)S(1)}, f32[1024]{0:T(1024)}, u32[]{:S(2)}) copy-start(f32[1024]{0:T(1024)} %copy-done.27) | copy-start | bytes 12292
  971.1 37.9 %copy-start.32 = (f32[512]{0:T(512)S(1)}, f32[512]{0:T(512)}, u32[]{:S(2)}) copy-start(f32[512]{0:T(512)} %copy-done.31) | copy-start | bytes 6148
  971.1 39.7 %copy-start.41 = (f32[512]{0:T(512)S(1)}, f32[512]{0:T(512)}, u32[]{:S(2)}) copy-start(f32[512]{0:T(512)} %copy-done.40) | copy-start | bytes 6148
  971.1 41.1 %copy-start.39 = (f32[512]{0:T(512)S(1)}, f32[512]{0:T(512)}, u32[]{:S(2)}) copy-start(f32[512]{0:T(512)} %copy-done.38) | copy-start | bytes 6148
  974.0 40.6 %copy-start.46 = (bf16[1024]{0:T(1024)(128)(2,1)S(1)}, bf16[1024]{0:T(1024)(128)(2,1)}, u32[]{:S(2)}) copy-start(bf16[1024]{0:T(1024)(128)(2,1)} %get-tuple-element.288) | copy-start | bytes 6148
  974.0 40.6 %copy-start.47 = (bf16[1024]{0:T(1024)(128)(2,1)S(1)}, bf16[1024]{0:T(1024)(128)(2,1)}, u32[]{:S(2)}) copy-start(bf16[1024]{0:T(1024)(128)(2,1)} %get-tuple-element.354) | copy-start | bytes 6148
  974.0 40.6 %copy-start.49 = (bf16[1024]{0:T(1024)(128)(2,1)S(1)}, bf16[1024]{0:T(1024)(128)(2,1)}, u32[]{:S(2)}) copy-start(bf16[1024]{0:T(1024)(128)(2,1)} %get-tuple-element.365) | copy-start | bytes 6148
  974.0 40.6 %copy-start.57 = (bf16[1024]{0:T(1024)(128)(2,1)S(1)}, bf16[1024]{0:T(1024)(128)(2,1)}, u32[]{:S(2)}) copy-start(bf16[1024]{0:T(1024)(128)(2,1)} %get-tuple-element.369) | copy-start | bytes 6148
  1052.5 18.2 %copy-start.1 = (bf16[1024,1024]{1,0:T(8,128)(2,1)S(1)}, bf16[1024,1024]{1,0:T(8,128)(2,1)}, u32[]{:S(2)}) copy-start(bf16[1024,1024]{1,0:T(8,128)(2,1)} %param.28) | copy-start | bytes 6291460
  (30 other events, 70.8 us)
Sparse Core Ops, SparseCore 0:
  15.3 37.1 all-gather.5
  140.0 44.4 reduce-scatter.4
  190.5 45.0 all-gather.7
  246.1 33.5 all-gather.9
  301.8 44.5 reduce-scatter.8
  348.7 44.4 reduce-scatter.6
  401.3 34.4 all-gather.11
  748.2 214.6 all-reduce.4
  965.5 43.4 reduce-scatter.10
